TPU v7x, 32 devices: a whole 2x2x4 slice. The times are simulated.
32 devices in a mesh: dp: 2 (over x), expert: 8 (over z, y), tensor: 2 (over core).
Axes of the slice: x: 2, y: 2, z: 4, core: 2. Of those that a mesh axis runs over, the one named last changes fastest.
Arguments:
- activations: bfloat16 [4096, 1536], P(('dp', 'expert', 'tensor')), may hold values from -6 to 6
- segments: int32 [16, 256], P(('dp', 'expert')), may hold values from 0 to 3, never falling along the last dimension, each value on 1 to 128 neighbouring positions
- routes: int32 [4096, 8], P(('dp', 'expert', 'tensor')), may hold values from 0 to 15, all different within a row; in each aligned block of 128 rows (0 to 127, 128 to 255, ...) at most 128 rows name the same one
- route_weights: float32 [4096, 8], P(('dp', 'expert', 'tensor')), may hold values from 0.03 to 0.3
- norm_attn_gain: float32 [1536], replicated, may hold values from 0.5 to 1.5
- norm_ffn_gain: float32 [1536], replicated, may hold values from 0.5 to 1.5
- query_weight: bfloat16 [1536, 1536], P(None, 'tensor'), may hold values from -0.15625 to 0.15625
- key_matrix: bfloat16 [1536, 512], P(None, 'tensor'), may hold values from -0.15625 to 0.15625
- value_matrix: bfloat16 [1536, 512], P(None, 'tensor'), may hold values from -0.15625 to 0.15625
- output_projection_weight: bfloat16 [1536, 1536], P('tensor'), may hold values from -0.625 to 0.625
- expert_gate: bfloat16 [16, 1536, 512], P('expert', None, 'tensor'), may hold values from -0.15625 to 0.15625
- expert_up: bfloat16 [16, 1536, 512], P('expert', None, 'tensor'), may hold values from -0.15625 to 0.15625
- expert_down: bfloat16 [16, 512, 1536], P('expert', 'tensor'), may hold values from -0.5 to 0.5
- grad_output: bfloat16 [4096, 1536], P(('dp', 'expert', 'tensor')), may hold values from -6 to 6
Outputs:
- block_out: bfloat16 [4096, 1536], P(('dp', 'expert', 'tensor'))
- grad_input: float32 [4096, 1536], P(('dp', 'expert', 'tensor'))
- grad_norm_attn: float32 [1536], replicated
- grad_norm_ffn: float32 [1536], replicated
- grad_query: float32 [1536, 1536], P(None, 'tensor')
- grad_key: float32 [1536, 512], P(None, 'tensor')
- grad_value: float32 [1536, 512], P(None, 'tensor')
- grad_mixer: float32 [1536, 1536], P('tensor')
- grad_expert_gate: float32 [16, 1536, 512], P('expert', None, 'tensor')
- grad_expert_up: float32 [16, 1536, 512], P('expert', None, 'tensor')
- grad_expert_down: float32 [16, 512, 1536], P('expert', 'tensor')
Inputs may be any that keep to these rules, and one draw needn't show every extreme that they name: `routes`: each row names 8 different experts; in the rows of one device (aligned blocks of 128 rows) no expert is named more than 128 times, and one is named exactly 128 times in some block. `segments`: each sequence's numbers never fall; 4 documents of 1 to 128 positions, one of exactly 128.
All inputs are finite; a program needn't handle non-finite values.
Results may differ from a plain program's by a relative error of at most 0.01.
Values may be sent and summed in bfloat16 or wider, within the bound.
No kernel may reach another device: no remote copies, remote signals or barrier semaphores. Data moves between devices by JAX's collectives and lax.ppermute only.
A program may use at most 320 MiB of HBM per device.

v0:
```python
import jax
import jax.numpy as jnp
from jax import lax
from jax.sharding import PartitionSpec as P

HEAD_DIM = 64
EPS = 1e-05
ATTN_SCALE = 0.015625
THETA = 10000.0
NEG_FILL = -1e30
F32 = jnp.float32
BF16 = jnp.bfloat16


def swap(values):
    return lax.ppermute(values, "tensor", [(0, 1), (1, 0)])


def norm_forward(values, gain_vector):
    inv_scale = lax.rsqrt(jnp.mean(values * values, axis=-1, keepdims=True) + EPS)
    return (values * inv_scale * gain_vector, inv_scale)


def norm_backward(values, inv_scale, gain_vector, upstream):
    weighted = upstream * gain_vector
    inner = jnp.mean(weighted * values, axis=-1, keepdims=True)
    value_gradient = inv_scale * weighted - values * (inv_scale * inv_scale * inv_scale) * inner
    grad_gain = jnp.sum(upstream * values * inv_scale, axis=0)
    return (value_gradient, grad_gain)


def rope_tables(position):
    frequency = THETA ** (-jnp.arange(HEAD_DIM // 2, dtype=F32) * 2.0 / HEAD_DIM)
    angle_table = position.astype(F32)[:, None] * frequency[None, :]
    return (jnp.cos(angle_table)[:, None, :], jnp.sin(angle_table)[:, None, :])


def rotate(field_in, cosine, sine):
    first, second = jnp.split(field_in, 2, axis=-1)
    return jnp.concatenate(
        [first * cosine - second * sine, second * cosine + first * sine], axis=-1
    )


def dot(spec, left, right):
    return jnp.einsum(spec, left, right, preferred_element_type=F32)


def body(
    activations,
    segments,
    routes,
    route_weights,
    norm_attn_gain,
    norm_ffn_gain,
    query_weight,
    key_matrix,
    value_matrix,
    output_projection_weight,
    expert_gate,
    expert_up,
    expert_down,
    grad_output,
):
    tensor_rank = lax.axis_index("tensor")
    rows, width = activations.shape
    experts_here = expert_gate.shape[0]
    expert_count = experts_here * lax.axis_size("expert")
    length = segments.shape[1]
    heads_q = query_weight.shape[1] // HEAD_DIM
    heads_kv = key_matrix.shape[1] // HEAD_DIM
    group = heads_q // heads_kv
    position = (jnp.arange(length, dtype=jnp.int32) + tensor_rank * rows) % length
    seg_ids = jnp.where(tensor_rank == 0, segments[0], jnp.roll(segments[0], rows))
    cosine, sine = rope_tables(position)
    allowed = (position[None, :] <= position[:, None]) & (seg_ids[None, :] == seg_ids[:, None])
    gate = jnp.concatenate([expert_gate, swap(expert_gate)], axis=2)
    up = jnp.concatenate([expert_up, swap(expert_up)], axis=2)
    down = jnp.concatenate([expert_down, swap(expert_down)], axis=1)
    upstream_all = lax.all_gather(grad_output, "expert", axis=0, tiled=True)
    named = routes[:, :, None] == jnp.arange(expert_count, dtype=jnp.int32)
    weight_table = jnp.sum(jnp.where(named, route_weights[:, :, None], 0.0), axis=1)
    weights_all = lax.all_gather(weight_table, "expert", axis=0, tiled=True)
    first_expert = lax.axis_index("expert") * experts_here
    weights_here = lax.dynamic_slice_in_dim(weights_all, first_expert, experts_here, 1).T
    x_in = jnp.concatenate([activations, swap(activations)], axis=0).astype(F32)
    normed_one, scale_one = norm_forward(x_in, norm_attn_gain)
    hidden_first = normed_one.astype(BF16)
    queries = dot("td,da->ta", hidden_first, query_weight).reshape(length, heads_q, HEAD_DIM)
    queries = rotate(queries, cosine, sine).astype(BF16).reshape(length, heads_kv, group, HEAD_DIM)
    keys = dot("td,da->ta", hidden_first, key_matrix).reshape(length, heads_kv, HEAD_DIM)
    keys = rotate(keys, cosine, sine).astype(BF16)
    value_rows = dot("td,da->ta", hidden_first, value_matrix).astype(BF16)
    value_rows = value_rows.reshape(length, heads_kv, HEAD_DIM)
    scores = jnp.where(allowed, dot("qhgd,khd->hgqk", queries, keys) * ATTN_SCALE, NEG_FILL)
    top_score = jnp.max(scores, axis=-1, keepdims=True)
    log_total = top_score + jnp.log(jnp.sum(jnp.exp(scores - top_score), axis=-1, keepdims=True))
    mixed = dot("hgqk,khd->qhgd", jnp.exp(scores - log_total).astype(BF16), value_rows).astype(BF16)
    mixed_flat = mixed.reshape(length, heads_q * HEAD_DIM)
    attn_part = dot("ta,ad->td", mixed_flat, output_projection_weight)
    residual = x_in[:rows] + attn_part[:rows] + swap(attn_part[rows:])
    normed_two, scale_two = norm_forward(residual, norm_ffn_gain)
    tokens_in = lax.all_gather(normed_two.astype(BF16), "expert", axis=0, tiled=True)
    pre_gate = dot("td,edf->etf", tokens_in, gate)
    pre_up = dot("td,edf->etf", tokens_in, up)
    gate_sigmoid = jax.nn.sigmoid(pre_gate)
    activated = (pre_gate * gate_sigmoid * pre_up).astype(BF16)
    expert_out = dot("etf,efd->etd", activated, down).astype(BF16)
    mix_part = jnp.sum(weights_here[:, :, None] * expert_out.astype(F32), axis=0).astype(BF16)
    grad_rows = (weights_here[:, :, None] * upstream_all.astype(F32)[None]).astype(BF16)
    grad_act = dot("etd,efd->etf", grad_rows, down)
    grad_pre_gate = (
        grad_act * pre_up * gate_sigmoid * (1.0 + pre_gate * (1.0 - gate_sigmoid))
    ).astype(BF16)
    grad_pre_up = (grad_act * pre_gate * gate_sigmoid).astype(BF16)
    grad_in = dot("etf,edf->etd", grad_pre_gate, gate) + dot("etf,edf->etd", grad_pre_up, up)
    grad_part = jnp.sum(weights_here[:, :, None] * grad_in, axis=0).astype(BF16)
    grad_h_own = lax.psum_scatter(grad_part, "expert", scatter_dimension=0, tiled=True)
    expert_mix = lax.psum_scatter(mix_part, "expert", scatter_dimension=0, tiled=True)
    block_out = (residual + expert_mix.astype(F32)).astype(BF16)

    def expert_sum(whole, axis):
        own, other = jnp.split(whole, 2, axis=axis)
        half = own + swap(other.astype(BF16)).astype(F32)
        return lax.psum(half.astype(BF16), "dp").astype(F32)

    gate_sum = expert_sum(dot("td,etf->edf", tokens_in, grad_pre_gate), 2)
    up_sum = expert_sum(dot("td,etf->edf", tokens_in, grad_pre_up), 2)
    down_sum = expert_sum(dot("etf,etd->efd", activated, grad_rows), 1)
    upstream_own = grad_output.astype(F32)
    grad_norm_part, grad_ffn_gain = norm_backward(
        residual, scale_two, norm_ffn_gain, grad_h_own.astype(F32)
    )
    grad_resid = upstream_own + grad_norm_part
    resid_own = grad_resid.astype(BF16)
    resid_full = jnp.concatenate([resid_own, swap(resid_own)], axis=0)
    grad_mix_w = dot("sa,sb->ab", mixed_flat, resid_full)
    mixed_grad = dot("im,dm->id", resid_full, output_projection_weight).astype(BF16)
    mixed_grad = mixed_grad.reshape(length, heads_kv, group, HEAD_DIM)
    probs = jnp.exp(scores - log_total)
    row_delta = dot("qhgd,qhgd->hgq", mixed_grad, mixed)
    grad_soft = dot("qhgd,khd->hgqk", mixed_grad, value_rows)
    grad_scores = (probs * (grad_soft - row_delta[..., None]) * ATTN_SCALE).astype(BF16)
    grad_queries = dot("hgqk,khd->qhgd", grad_scores, keys)
    grad_keys = dot("hgqk,qhgd->khd", grad_scores, queries)
    grad_values = dot("hgqk,qhgd->khd", probs.astype(BF16), mixed_grad)
    grad_q_rows = rotate(grad_queries.reshape(length, heads_q, HEAD_DIM), cosine, -sine)
    grad_q_rows = grad_q_rows.astype(BF16).reshape(length, -1)
    grad_k_rows = rotate(grad_keys, cosine, -sine).astype(BF16).reshape(length, -1)
    grad_v_rows = grad_values.astype(BF16).reshape(length, -1)
    grad_q_w = dot("sd,sa->da", hidden_first, grad_q_rows)
    grad_k_w = dot("sd,sa->da", hidden_first, grad_k_rows)
    grad_v_w = dot("sd,sa->da", hidden_first, grad_v_rows)
    grad_h_part = (
        dot("sa,da->sd", grad_q_rows, query_weight)
        + dot("sa,da->sd", grad_k_rows, key_matrix)
        + dot("sa,da->sd", grad_v_rows, value_matrix)
    )
    grad_h_one = grad_h_part[:rows] + swap(grad_h_part[rows:])
    grad_x_part, grad_attn_gain = norm_backward(
        x_in[:rows], scale_one[:rows], norm_attn_gain, grad_h_one
    )
    grad_input = grad_resid + grad_x_part
    dense = [t.astype(BF16) for t in (grad_q_w, grad_k_w, grad_v_w, grad_mix_w)]
    dense = [t.astype(F32) for t in lax.psum(dense, ("dp", "expert"))]
    gains = lax.psum(jnp.stack([grad_attn_gain, grad_ffn_gain]), ("dp", "expert", "tensor"))
    return (block_out, grad_input, gains[0], gains[1], *dense, gate_sum, up_sum, down_sum)


def solution(mesh):
    tokens = P(("dp", "expert", "tensor"), None)
    whole = P()
    columns = P(None, "tensor")
    hidden_last = P("expert", None, "tensor")
    hidden_mid = P("expert", "tensor", None)
    mixer = P("tensor", None)
    return jax.shard_map(
        body,
        mesh=mesh,
        in_specs=(
            tokens,
            P(("dp", "expert"), None),
            tokens,
            tokens,
            whole,
            whole,
            columns,
            columns,
            columns,
            mixer,
            hidden_last,
            hidden_last,
            hidden_mid,
            tokens,
        ),
        out_specs=(
            tokens,
            tokens,
            whole,
            whole,
            columns,
            columns,
            columns,
            mixer,
            hidden_last,
            hidden_last,
            hidden_mid,
        ),
        check_vma=False,
    )
```

profile of v0, /device:TPU:0, one launch (start us, length us, event | category | flops | bytes accessed | tf_op | source)
XLA Modules:
  0.0 691.7 jit_solution(6405158610316332684)
XLA Ops:
  13.1 1.8 fusion.64
  22.1 2.1 collective-permute-done.1
  26.6 2.6 copy.79
  29.6 2.6 copy.77
  32.3 32.2 %all_gather.9 = f32[1024,16]{0,1:T(8,128)S(1)} all-gather(f32[128,16]{0,1:T(8,128)S(1)} %select_reduce_fusion), channel_id=1, replica_groups=mesh['dp'=2,'expert'=8,'tensor'=2] {'expert'}, dimensions={0}, use_global_device_ids=true | all-gather | bytes 73728 | tf_op jit(solution)/shard_map/all_gather | solution.py:83
  64.6 2.7 constant_dynamic-update-slice_fusion.1
  67.2 2.7 constant_dynamic-update-slice_fusion
  69.9 4.5 all-gather.5.cloned.1.call-done
  74.3 5.4 convert_element_type.165
  79.7 56.4 %all-gather.3.cloned.1.call-done = bf16[1024,1536]{1,0:T(8,128)(2,1)} async-done(((bf16[128,1536]{1,0:T(8,128)(2,1)}), bf16[1024,1536]{1,0:T(8,128)(2,1)}) %all-gather.3.cloned.1.call-update) | async-done | bytes 3145744 | tf_op jit(solution)/shard_map/all_gather | solution.py:103
  136.1 6.9 %fusion.24 = f32[2,512,1024]{2,1,0:T(8,128)S(1)} fusion(bf16[1024,1536]{1,0:T(8,128)(2,1)} %all-gather.3.cloned.1.call-done, bf16[2,1536,256]{1,2,0:T(8,128)(2,1)} %collective-permute-done.3, bf16[2,1536,256]{1,2,0:T(8,128)(2,1)} %copy.79), kind=kOutput, calls=%fused_computation.46 | convolution fusion | flops 3227516928 | bytes 10485760 | tf_op jit(solution)/shard_map/td,edf->etf/dot_general | solution.py:46
  143.1 6.5 fusion.26
  149.7 9.5 %fusion.9 = (bf16[2,1024,512]{1,2,0:T(8,128)(2,1)}, bf16[2,1024,512]{1,2,0:T(8,128)(2,1)}, bf16[2,1024,512]{1,2,0:T(8,128)(2,1)S(1)}) fusion(f32[2,512,1024]{2,1,0:T(8,128)S(1)} %fusion.24, f32[2,512,1024]{2,1,0:T(8,128)} %fusion.26, bf16[2,512,1536]{2,1,0:T(8,128)(2,1)} %constant_dynamic-update-slice_fusion, f32[1024,1536]{1,0:T(8,128)S(1)} %bitcast.160, ...), kind=kOutput, calls=%fused_computation.16 | convolution fusion | flops 3244294144 | bytes 24125440 | tf_op jit(solution)/shard_map/etd,efd->etf/dot_general | solution.py:46
  159.1 8.6 %fusion.30 = f32[2,1024,1536]{2,1,0:T(8,128)} fusion(bf16[2,1024,512]{1,2,0:T(8,128)(2,1)S(1)} %get-tuple-element.61, bf16[2,1536,256]{1,2,0:T(8,128)(2,1)} %collective-permute-done.3, bf16[2,1536,256]{1,2,0:T(8,128)(2,1)S(1)} %copy-done.11), kind=kOutput, calls=%fused_computation.59 | convolution fusion | flops 3227516928 | bytes 17825792 | tf_op jit(solution)/shard_map/etf,edf->etd/dot_general | solution.py:46
  167.7 13.0 %multiply_reduce_fusion = bf16[1024,1536]{1,0:T(8,128)(2,1)} fusion(f32[2,1024,1536]{2,1,0:T(8,128)} %fusion.30, f32[2,1024]{1,0:T(2,128)S(1)} %dynamic-slice_bitcast_fusion, bf16[2,1024,512]{1,2,0:T(8,128)(2,1)} %get-tuple-element.59, bf16[2,1536,256]{1,2,0:T(8,128)(2,1)} %collective-permute-done.2, bf16[2,1536,256]{1,2,0:T(8,128)(2,1)} %copy.77), kind=kOutput, calls=%fused_computation | convolution fusion | flops 3235381248 | bytes 20979712 | tf_op jit(solution)/shard_map/etf,edf->etd/dot_general | solution.py:46
  181.0 7.1 %fusion = f32[2,512,1536]{2,1,0:T(8,128)S(1)} fusion(bf16[2,1024,512]{1,2,0:T(8,128)(2,1)} %get-tuple-element.60, f32[1024,1536]{1,0:T(8,128)} %convert_element_type.165, f32[2,1024]{1,0:T(2,128)S(1)} %dynamic-slice_bitcast_fusion), kind=kOutput, calls=%fused_computation.3 | convolution fusion | flops 3227516928 | bytes 14688256 | tf_op jit(solution)/shard_map/etf,etd->efd/dot_general | solution.py:46
  188.4 1.6 copy-done.62
  190.0 3.4 convolution_bitcast_fusion.1
  195.0 3.4 convolution_bitcast_fusion
  198.7 1.6 fusion.16
  200.3 1.8 fusion.18
  202.1 1.6 fusion.17
  203.8 8.9 %multiply_reduce_fusion.1 = bf16[1024,1536]{1,0:T(8,128)(2,1)} fusion(f32[2,1024]{1,0:T(2,128)S(1)} %dynamic-slice_bitcast_fusion, bf16[2,1024,512]{1,2,0:T(8,128)(2,1)} %get-tuple-element.60, bf16[2,512,1536]{2,1,0:T(8,128)(2,1)} %constant_dynamic-update-slice_fusion), kind=kOutput, calls=%fused_computation.2 | convolution fusion | flops 3232235520 | bytes 8396800 | tf_op jit(solution)/shard_map/etf,efd->etd/dot_general | solution.py:46
  212.9 41.2 %reduce-scatter.5.cloned.1.call-done = bf16[128,1536]{1,0:T(8,128)(2,1)} async-done(((bf16[1024,1536]{1,0:T(8,128)(2,1)}), bf16[128,1536]{1,0:T(8,128)(2,1)}) %reduce-scatter.5.cloned.1.call-update) | async-done | bytes 393232 | tf_op jit(solution)/shard_map/reduce_scatter | solution.py:118
  254.1 1.8 fusion.38
  256.0 1.4 fusion.62
  257.5 1.7 collective-permute-done.5
  259.9 1.6 convolution_convert_fusion.5
  261.5 2.0 copy.87
  264.6 3.2 fusion.21
  269.7 1.4 convolution_convert_fusion.3
  272.4 1.4 convolution_convert_fusion.2
  273.8 2.2 convolution_convert_fusion
  276.0 2.3 convolution_convert_fusion.1
  279.3 2.6 fusion.68
  287.1 88.6 %all-reduce.7.cloned.1.call-done = (bf16[2,1536,256]{1,2,0:T(8,128)(2,1)}, bf16[2,1536,256]{1,2,0:T(8,128)(2,1)}, bf16[2,256,1536]{2,1,0:T(8,128)(2,1)}) async-done(((bf16[2,1536,256]{1,2,0:T(8,128)(2,1)}, bf16[2,1536,256]{1,2,0:T(8,128)(2,1)}, bf16[2,256,1536]{2,1,0:T(8,128)(2,1)}), (bf16[2,1536,256]{1,2,0:T(8,128)(2,1)}, bf16[2,1536,256]{1,2,0:T(8,128)(2,1)}, ...) | async-done | bytes 4718608 | tf_op jit(solution)/shard_map/psum | solution.py:125
  375.8 3.1 copy.91
  378.8 3.1 copy.92
  381.9 3.6 convert_element_type.194
  385.6 1.9 multiply_reduce_fusion.3
  388.2 40.9 %psum.56 = f32[2,1536]{1,0:T(2,128)} all-reduce(f32[2,1536]{1,0:T(2,128)} %pad_maximum_fusion.14), channel_id=1, replica_groups=mesh['dp'=2,'expert'=8,'tensor'=2] {'dp','expert','tensor'}, use_global_device_ids=true, to_apply=%region_13.14 | all-reduce | flops 3072 | bytes 24576 | tf_op jit(solution)/shard_map/psum | solution.py:166
  429.0 1.4 slice_reduce_fusion
  431.6 24.1 %reduce-scatter.3.cloned.1.call-done = bf16[128,1536]{1,0:T(8,128)(2,1)} async-done(((bf16[1024,1536]{1,0:T(8,128)(2,1)}), bf16[128,1536]{1,0:T(8,128)(2,1)}) %reduce-scatter.3.cloned.1.call-update) | async-done | bytes 393232 | tf_op jit(solution)/shard_map/reduce_scatter | solution.py:119
  455.7 3.3 subtract_add_fusion
  459.0 216.4 %all-reduce.5.cloned.1.call-done = (bf16[1536,768]{1,0:T(8,128)(2,1)}, bf16[1536,256]{1,0:T(8,128)(2,1)}, bf16[1536,256]{1,0:T(8,128)(2,1)}, bf16[768,1536]{1,0:T(8,128)(2,1)}) async-done(((bf16[1536,768]{1,0:T(8,128)(2,1)}, bf16[1536,256]{1,0:T(8,128)(2,1)}, bf16[1536,256]{1,0:T(8,128)(2,1)}, bf16[768,1536]{1,0:T(8,128)(2,1)}), (bf16[1536,768]{1,0:T(8,128)(2,1)}, bf16[1536,256]{1,0:T(8,128)(2,1)}, ...) | async-done | bytes 6291472 | tf_op jit(solution)/shard_map/psum | solution.py:165
  675.5 2.5 convert_element_type.181
  679.3 2.5 convert_element_type.179
  681.8 2.8 convert_element_type.185
  (215 shorter events, 32.6 us)
Async XLA Ops:
  7.2 13.7 %copy-start = (bf16[768,1536]{1,0:T(8,128)(2,1)S(1)}, bf16[768,1536]{1,0:T(8,128)(2,1)}, u32[]{:S(2)}) copy-start(bf16[768,1536]{1,0:T(8,128)(2,1)} %param.23) | copy-start | bytes 7077892
  7.2 7.8 %copy-start.13 = (bf16[128,1536]{1,0:T(8,128)(2,1)S(1)}, bf16[128,1536]{1,0:T(8,128)(2,1)}, u32[]{:S(2)}) copy-start(bf16[128,1536]{1,0:T(8,128)(2,1)} %param.14) | copy-start | bytes 1179652
  7.2 7.8 %copy-start.46 = (f32[1536]{0:T(1024)S(1)}, f32[1536]{0:T(1024)}, u32[]{:S(2)}) copy-start(f32[1536]{0:T(1024)} %param.18) | copy-start | bytes 18436
  7.2 67.1 %all-gather.5.cloned.1.call-start = ((), (), s32[]{:S(2)}) async-start(), calls=%async_computation.4 | async-start | bytes 3538944 | tf_op jit(solution)/shard_map/all_gather | solution.py:80
  8.0 128.2 %all-gather.3.cloned.1.call-start = ((), (), s32[]{:S(2)}) async-start(), calls=%async_computation.2 | async-start | bytes 3538944 | tf_op jit(solution)/shard_map/all_gather | solution.py:103
  8.0 3.7 collective-permute-start
  8.5 6.5 copy-start.10
  10.9 9.1 %copy-start.41 = (pred[256,256]{0,1:T(8,128)(4,1)}, pred[256,256]{0,1:T(8,128)(4,1)S(1)}, u32[]{:S(2)}) copy-start(pred[256,256]{0,1:T(8,128)(4,1)S(1)} %compare_and_fusion) | copy-start | bytes 196612
  11.7 4.5 copy-start.22
  11.7 10.1 %copy-start.15 = (bf16[128,1536]{1,0:T(8,128)(2,1)}, bf16[128,1536]{1,0:T(8,128)(2,1)S(1)}, u32[]{:S(2)}) copy-start(bf16[128,1536]{1,0:T(8,128)(2,1)S(1)} %collective-permute-done) | copy-start | bytes 1179652
  13.1 5.3 copy-start.58
  21.8 3.7 copy-start.43
  21.8 2.4 collective-permute-start.1
  26.4 227.7 %reduce-scatter.5.cloned.1.call-start = ((), (), s32[]{:S(2)}) async-start(), calls=%async_computation.5 | async-start | bytes 3538944 | tf_op jit(solution)/shard_map/reduce_scatter | solution.py:118
  26.4 40.8 %collective-permute-start.4 = (bf16[2,256,1536]{2,1,0:T(8,128)(2,1)}, bf16[2,256,1536]{2,1,0:T(8,128)(2,1)}, u32[]{:S(2)}, u32[]{:S(2)}) collective-permute-start(bf16[2,256,1536]{2,1,0:T(8,128)(2,1)} %param.26), channel_id=1, source_target_pairs={{0,1},{1,0},{2,3},{3,2},{4,5},{5,4},{6,7},{7,6},{8,9},{9,8},{10,11... | collective-permute-start | bytes 4718600 | tf_op jit(solution)/shard_map/ppermute | solution.py:16
  29.2 3.1 copy-start.53
  29.2 3.1 copy-start.54
  29.2 50.5 %collective-permute-start.3 = (bf16[2,1536,256]{1,2,0:T(8,128)(2,1)}, bf16[2,1536,256]{1,2,0:T(8,128)(2,1)}, u32[]{:S(2)}, u32[]{:S(2)}) collective-permute-start(bf16[2,1536,256]{1,2,0:T(8,128)(2,1)} %copy.79), channel_id=1, source_target_pairs={{0,1},{1,0},{2,3},{3,2},{4,5},{5,4},{6,7},{7,6},{8,9},{9,8},{10,11... | collective-permute-start | bytes 4718600 | tf_op jit(solution)/shard_map/ppermute | solution.py:16
  32.2 110.9 %collective-permute-start.2 = (bf16[2,1536,256]{1,2,0:T(8,128)(2,1)}, bf16[2,1536,256]{1,2,0:T(8,128)(2,1)}, u32[]{:S(2)}, u32[]{:S(2)}) collective-permute-start(bf16[2,1536,256]{1,2,0:T(8,128)(2,1)} %copy.77), channel_id=1, source_target_pairs={{0,1},{1,0},{2,3},{3,2},{4,5},{5,4},{6,7},{7,6},{8,9},{9,8},{10,11... | collective-permute-start | bytes 4718600 | tf_op jit(solution)/shard_map/ppermute | solution.py:16
  136.1 7.0 %copy-start.12 = (bf16[2,1536,256]{1,2,0:T(8,128)(2,1)S(1)}, bf16[2,1536,256]{1,2,0:T(8,128)(2,1)}, u32[]{:S(2)}) copy-start(bf16[2,1536,256]{1,2,0:T(8,128)(2,1)} %copy.77) | copy-start | bytes 4718596
  136.1 7.0 %copy-start.61 = (bf16[1024,1536]{1,0:T(8,128)(2,1)S(1)}, bf16[1024,1536]{1,0:T(8,128)(2,1)}, u32[]{:S(2)}) copy-start(bf16[1024,1536]{1,0:T(8,128)(2,1)} %all-gather.3.cloned.1.call-done) | copy-start | bytes 9437188
  136.1 13.5 %slice-start = ((s8[6291456]{0:T(1024)(128)(4,1)}), s8[4194304]{0:T(1024)(128)(4,1)S(1)}, s32[]{:S(2)}) async-start(s8[6291456]{0:T(1024)(128)(4,1)} %bitcast.159), calls=%async_computation.8 | async-start | bytes 8388608
  143.1 6.6 slice-start.1
  149.6 9.5 %copy-start.11 = (bf16[2,1536,256]{1,2,0:T(8,128)(2,1)S(1)}, bf16[2,1536,256]{1,2,0:T(8,128)(2,1)}, u32[]{:S(2)}) copy-start(bf16[2,1536,256]{1,2,0:T(8,128)(2,1)} %copy.79) | copy-start | bytes 4718596
  159.1 8.6 %copy-start.64 = (bf16[2,1024,512]{1,2,0:T(8,128)(2,1)}, bf16[2,1024,512]{1,2,0:T(8,128)(2,1)S(1)}, u32[]{:S(2)}) copy-start(bf16[2,1024,512]{1,2,0:T(8,128)(2,1)S(1)} %get-tuple-element.61) | copy-start | bytes 6291460
  180.8 195.0 %all-reduce.7.cloned.1.call-start = ((), (), s32[]{:S(2)}) async-start(), calls=%async_computation.7 | async-start | bytes 9437184 | tf_op jit(solution)/shard_map/psum | solution.py:125
  181.0 7.3 %copy-start.66 = (bf16[2,1024,512]{1,2,0:T(8,128)(2,1)S(1)}, bf16[2,1024,512]{1,2,0:T(8,128)(2,1)}, u32[]{:S(2)}) copy-start(bf16[2,1024,512]{1,2,0:T(8,128)(2,1)} %get-tuple-element.59) | copy-start | bytes 6291460
  188.3 10.4 %collective-permute-start.9 = (bf16[2,256,1536]{2,1,0:T(8,128)(2,1)S(1)}, bf16[2,256,1536]{2,1,0:T(8,128)(2,1)S(1)}, u32[]{:S(2)}, u32[]{:S(2)}) collective-permute-start(bf16[2,256,1536]{2,1,0:T(8,128)(2,1)S(1)} %split.101), channel_id=1, source_target_pairs={{0,1},{1,0},{2,3},{3,2},{4,5},{5,4},{6,7},{7,6},{8,9},{9,8},{10,11... | collective-permute-start | bytes 4718600 | tf_op jit(solution)/shard_map/ppermute | solution.py:16
  193.6 6.7 collective-permute-start.7
  198.6 3.5 collective-permute-start.8
  203.7 252.0 %reduce-scatter.3.cloned.1.call-start = ((), (), s32[]{:S(2)}) async-start(), calls=%async_computation.3 | async-start | bytes 3538944 | tf_op jit(solution)/shard_map/reduce_scatter | solution.py:119
  212.6 41.5 %copy-start.52 = (f32[128]{0:T(128)S(1)}, f32[128]{0:T(128)}, u32[]{:S(2)}) copy-start(f32[128]{0:T(128)} %copy-done.51) | copy-start | bytes 1540
  212.6 43.3 %copy-start.56 = (f32[128]{0:T(128)S(1)}, f32[128]{0:T(128)}, u32[]{:S(2)}) copy-start(f32[128]{0:T(128)} %get-tuple-element.79) | copy-start | bytes 1540
  212.6 462.8 %all-reduce.5.cloned.1.call-start = ((), (), s32[]{:S(2)}) async-start(), calls=%async_computation.6 | async-start | bytes 12582912 | tf_op jit(solution)/shard_map/psum | solution.py:165
  257.4 1.8 collective-permute-start.5
  264.6 3.3 copy-start.25
  264.6 3.3 copy-start.27
  264.6 3.9 copy-start.23
  264.6 3.9 copy-start.36
  269.3 6.7 copy-start.18
  272.4 3.6 copy-start.44
  285.6 100.0 %collective-permute-start.6 = (f32[128,1536]{1,0:T(8,128)}, f32[128,1536]{1,0:T(8,128)}, u32[]{:S(2)}, u32[]{:S(2)}) collective-permute-start(f32[128,1536]{1,0:T(8,128)} %slice.53), channel_id=1, source_target_pairs={{0,1},{1,0},{2,3},{3,2},{4,5},{5,4},{6,7},{7,6},{8,9},{9,8},{10,11... | collective-permute-start | bytes 2359304 | tf_op jit(solution)/shard_map/ppermute | solution.py:16
  381.9 3.6 copy-start.48
  381.9 3.7 copy-start.2
  381.9 3.7 copy-start.4
  381.9 3.7 copy-start.55
  385.6 70.2 %copy-start.5 = (bf16[128,1536]{1,0:T(8,128)(2,1)S(1)}, bf16[128,1536]{1,0:T(8,128)(2,1)}, u32[]{:S(2)}) copy-start(bf16[128,1536]{1,0:T(8,128)(2,1)} %param.27) | copy-start | bytes 1179652
  675.5 3.8 copy-start.9
  (37 other events, 58.4 us)
Sparse Core Ops, SparseCore 0:
  10.2 64.0 all-gather.4
  77.1 58.9 all-gather.2
  180.9 73.1 reduce-scatter.4
  256.6 119.1 all-reduce.6
  380.2 75.4 reduce-scatter.2
  463.7 211.6 all-reduce.4
where the time goes:
time: 699 us; the launch traced here: 692 us
  waiting for transfers between devices  436 us (62%)
  matrix products  90.5 us (13%)
  blocking collectives  73.1 us (10%)
  other arithmetic  41.7 us (6%)
  local copies, waits for them, and re-layouts  32.8 us (5%)
  between operations  15.2 us (2%)
    psum x1, waiting for transfers between devices, body(): dense = [t.astype(F32) for t in lax.psum(dense, ('dp', 'expert'))]  216 us
    dot_general x27, matrix products, dot(): return jnp.einsum(spec, left, right, preferred_element_type=F32)  90.5 us
    psum x1, waiting for transfers between devices, expert_sum(): return lax.psum(half.astype(BF16), 'dp').astype(F32)  88.6 us
    all_gather x1, waiting for transfers between devices, body(): lax.all_gather(normed_two.astype(BF16), 'expert', axis=0, tiled=True)  56.4 us
    reduce_scatter x1, waiting for transfers between devices, body(): lax.psum_scatter(grad_part, 'expert', scatter_dimension=0, tiled=True)  41.2 us
    psum x1, blocking collectives, body(): lax.psum(jnp.stack([grad_attn_gain, grad_ffn_gain]), ('dp', 'expert', 'te...  40.9 us
    all_gather x1, blocking collectives, body(): weights_all = lax.all_gather(weight_table, 'expert', axis=0, tiled=True)  32.2 us
    reduce_scatter x1, waiting for transfers between devices, body(): lax.psum_scatter(mix_part, 'expert', scatter_dimension=0, tiled=True)  24.1 us
  transfers between devices with their start and end apart: 16, of which 8 were waited for; matrix products, arithmetic and copies ran while one was open for 16% of the time, Pallas kernels for 0%

commit v1 on v0

--- a/solution.py
+++ b/solution.py
@@ -162,7 +162,7 @@
     )
     grad_input = grad_resid + grad_x_part
     dense = [t.astype(BF16) for t in (grad_q_w, grad_k_w, grad_v_w, grad_mix_w)]
-    dense = [t.astype(F32) for t in lax.psum(dense, ("dp", "expert"))]
+    dense = [t.astype(F32) for t in lax.psum(lax.psum(dense, "expert"), "dp")]
     gains = lax.psum(jnp.stack([grad_attn_gain, grad_ffn_gain]), ("dp", "expert", "tensor"))
     return (block_out, grad_input, gains[0], gains[1], *dense, gate_sum, up_sum, down_sum)
 

time: 699 us -> 861 us (1.23)
  waiting for transfers between devices: 436 us -> 608 us
    psum x1, waiting for transfers between devices: 88.6 us -> 258 us  [expert_sum(): return lax.psum(half.astype(BF16), 'dp').astype(F32)]
    psum x1, waiting for transfers between devices: 216 us -> 181 us  [body(): dense = [t.astype(F32) for t in lax.psum(lax.psum(dense, 'expert'), 'dp')]]
    reduce_scatter x1, waiting for transfers between devices: 41.2 us -> 73 us  [body(): lax.psum_scatter(grad_part, 'expert', scatter_dimension=0, tiled=True)]
    unnamed x143 -> x153, local copies, waits for them, and re-layouts: 23.8 us -> 22.1 us
  transfers between devices with their start and end apart: 16 -> 16, of which waited for: 8 -> 9; matrix products, arithmetic and copies ran while one was open for 16% -> 8% of each run, Pallas kernels for 0% -> 0%
where the time goes in v1:
time: 861 us; the launch traced here: 854 us
  waiting for transfers between devices  608 us (71%)
  matrix products  89.1 us (10%)
  blocking collectives  73.3 us (9%)
  other arithmetic  36.8 us (4%)
  local copies, waits for them, and re-layouts  27.9 us (3%)
  between operations  15.3 us (2%)
    psum x1, waiting for transfers between devices, expert_sum(): return lax.psum(half.astype(BF16), 'dp').astype(F32)  258 us
    psum x1, waiting for transfers between devices, body(): dense = [t.astype(F32) for t in lax.psum(lax.psum(dense, 'expert'), 'dp')]  181 us
    dot_general x27, matrix products, dot(): return jnp.einsum(spec, left, right, preferred_element_type=F32)  89.1 us
    reduce_scatter x1, waiting for transfers between devices, body(): lax.psum_scatter(grad_part, 'expert', scatter_dimension=0, tiled=True)  73 us
    all_gather x1, waiting for transfers between devices, body(): lax.all_gather(normed_two.astype(BF16), 'expert', axis=0, tiled=True)  56.5 us
    psum x1, blocking collectives, body(): lax.psum(jnp.stack([grad_attn_gain, grad_ffn_gain]), ('dp', 'expert', 'te...  40.6 us
    all_gather x1, blocking collectives, body(): weights_all = lax.all_gather(weight_table, 'expert', axis=0, tiled=True)  32.7 us
    reduce_scatter x1, waiting for transfers between devices, body(): lax.psum_scatter(mix_part, 'expert', scatter_dimension=0, tiled=True)  28.9 us
  transfers between devices with their start and end apart: 16, of which 9 were waited for; matrix products, arithmetic and copies ran while one was open for 8% of the time, Pallas kernels for 0%

profile of v1, /device:TPU:0, one launch (start us, length us, event | category | flops | bytes accessed | tf_op | source)
XLA Modules:
  0.0 853.7 jit_solution(3887493215445191323)
XLA Ops:
  11.2 1.4 multiply_reduce_fusion.2
  12.6 1.8 fusion.64
  21.6 2.1 collective-permute-done.1
  26.2 2.6 copy.77
  29.1 2.6 copy.79
  31.9 32.7 %all_gather.9 = f32[1024,16]{0,1:T(8,128)S(1)} all-gather(f32[128,16]{0,1:T(8,128)S(1)} %select_reduce_fusion), channel_id=1, replica_groups=mesh['dp'=2,'expert'=8,'tensor'=2] {'expert'}, dimensions={0}, use_global_device_ids=true | all-gather | bytes 73728 | tf_op jit(solution)/shard_map/all_gather | solution.py:83
  64.6 2.7 constant_dynamic-update-slice_fusion.1
  67.2 2.7 constant_dynamic-update-slice_fusion
  69.9 4.5 all-gather.5.cloned.1.call-done
  74.3 5.4 convert_element_type.165
  79.7 56.5 %all-gather.3.cloned.1.call-done = bf16[1024,1536]{1,0:T(8,128)(2,1)} async-done(((bf16[128,1536]{1,0:T(8,128)(2,1)}), bf16[1024,1536]{1,0:T(8,128)(2,1)}) %all-gather.3.cloned.1.call-update) | async-done | bytes 3145744 | tf_op jit(solution)/shard_map/all_gather | solution.py:103
  136.2 6.8 fusion.26
  143.1 6.5 fusion.24
  149.6 9.3 %fusion.9 = (bf16[2,1024,512]{1,2,0:T(8,128)(2,1)}, bf16[2,1024,512]{1,2,0:T(8,128)(2,1)}, bf16[2,1024,512]{1,2,0:T(8,128)(2,1)S(1)}) fusion(f32[2,512,1024]{2,1,0:T(8,128)} %fusion.24, f32[2,512,1024]{2,1,0:T(8,128)S(1)} %fusion.26, bf16[2,512,1536]{2,1,0:T(8,128)(2,1)} %constant_dynamic-update-slice_fusion, f32[1024,1536]{1,0:T(8,128)S(1)} %bitcast.160, ...), kind=kOutput, calls=%fused_computation.16 | convolution fusion | flops 3244294144 | bytes 24125440 | tf_op jit(solution)/shard_map/etd,efd->etf/dot_general | solution.py:46
  158.9 8.6 %fusion.30 = f32[2,1024,1536]{2,1,0:T(8,128)} fusion(bf16[2,1024,512]{1,2,0:T(8,128)(2,1)S(1)} %get-tuple-element.65, bf16[2,1536,256]{1,2,0:T(8,128)(2,1)} %collective-permute-done.3, bf16[2,1536,256]{1,2,0:T(8,128)(2,1)S(1)} %copy-done.13), kind=kOutput, calls=%fused_computation.59 | convolution fusion | flops 3227516928 | bytes 17825792 | tf_op jit(solution)/shard_map/etf,edf->etd/dot_general | solution.py:46
  167.5 13.0 %multiply_reduce_fusion = bf16[1024,1536]{1,0:T(8,128)(2,1)} fusion(f32[2,1024,1536]{2,1,0:T(8,128)} %fusion.30, f32[2,1024]{1,0:T(2,128)S(1)} %dynamic-slice_bitcast_fusion, bf16[2,1024,512]{1,2,0:T(8,128)(2,1)} %get-tuple-element.63, bf16[2,1536,256]{1,2,0:T(8,128)(2,1)} %collective-permute-done.2, bf16[2,1536,256]{1,2,0:T(8,128)(2,1)} %copy.77), kind=kOutput, calls=%fused_computation | convolution fusion | flops 3235381248 | bytes 20979712 | tf_op jit(solution)/shard_map/etf,edf->etd/dot_general | solution.py:46
  180.8 73.0 %reduce-scatter.5.cloned.1.call-done = bf16[128,1536]{1,0:T(8,128)(2,1)} async-done(((bf16[1024,1536]{1,0:T(8,128)(2,1)}), bf16[128,1536]{1,0:T(8,128)(2,1)}) %reduce-scatter.5.cloned.1.call-update) | async-done | bytes 393232 | tf_op jit(solution)/shard_map/reduce_scatter | solution.py:118
  253.8 1.8 fusion.38
  255.7 1.4 fusion.62
  257.2 1.7 collective-permute-done.5
  259.6 1.6 convolution_convert_fusion.5
  262.4 2.9 fusion.31
  268.4 2.2 convolution_convert_fusion
  270.6 1.4 convolution_convert_fusion.2
  272.1 1.4 convolution_convert_fusion.3
  273.5 2.3 convolution_convert_fusion.1
  275.9 1.5 copy-done.12
  277.4 8.3 multiply_reduce_fusion.1
  286.0 6.5 fusion
  292.9 1.5 copy-done.66
  294.4 3.4 convolution_bitcast_fusion
  299.4 3.4 convolution_bitcast_fusion.1
  303.3 1.8 fusion.16
  305.0 1.7 fusion.17
  306.7 1.6 fusion.18
  308.4 181.1 %all-reduce.5.cloned.1.call-done = (bf16[1536,768]{1,0:T(8,128)(2,1)}, bf16[1536,256]{1,0:T(8,128)(2,1)}, bf16[1536,256]{1,0:T(8,128)(2,1)}, bf16[768,1536]{1,0:T(8,128)(2,1)}) async-done(((bf16[1536,768]{1,0:T(8,128)(2,1)}, bf16[1536,256]{1,0:T(8,128)(2,1)}, bf16[1536,256]{1,0:T(8,128)(2,1)}, bf16[768,1536]{1,0:T(8,128)(2,1)}), (bf16[1536,768]{1,0:T(8,128)(2,1)}, bf16[1536,256]{1,0:T(8,128)(2,1)}, ...) | async-done | bytes 6291472 | tf_op jit(solution)/shard_map/psum | solution.py:165
  490.5 2.6 fusion.68
  495.0 2.2 collective-permute-done.6
  498.1 40.6 %psum.84 = f32[2,1536]{1,0:T(2,128)S(1)} all-reduce(f32[2,1536]{1,0:T(2,128)S(1)} %pad_maximum_fusion.14), channel_id=1, replica_groups=mesh['dp'=2,'expert'=8,'tensor'=2] {'dp','expert','tensor'}, use_global_device_ids=true, to_apply=%region_13.14 | all-reduce | flops 3072 | bytes 24576 | tf_op jit(solution)/shard_map/psum | solution.py:166
  539.3 28.9 %reduce-scatter.3.cloned.1.call-done = bf16[128,1536]{1,0:T(8,128)(2,1)} async-done(((bf16[1024,1536]{1,0:T(8,128)(2,1)}), bf16[128,1536]{1,0:T(8,128)(2,1)}) %reduce-scatter.3.cloned.1.call-update) | async-done | bytes 393232 | tf_op jit(solution)/shard_map/reduce_scatter | solution.py:119
  568.3 2.9 subtract_add_fusion
  571.2 258.2 %all-reduce.7.cloned.1.call-done = (bf16[2,1536,256]{1,2,0:T(8,128)(2,1)}, bf16[2,1536,256]{1,2,0:T(8,128)(2,1)}, bf16[1536,768]{1,0:T(8,128)(2,1)}, bf16[1536,2...) async-done(((bf16[2,1536,256]{1,2,0:T(8,128)(2,1)}, bf16[2,1536,256]{1,2,0:T(8,128)(2,1)}, ...) | async-done | bytes 11010064 | tf_op jit(solution)/shard_map/psum | solution.py:125
  829.4 4.4 convert_element_type.179
  833.8 2.8 convert_element_type.185
  836.6 2.1 convert_element_type.194
  838.7 2.1 copy.91
  840.8 2.1 copy.92
  842.8 2.5 convert_element_type.181
  (225 shorter events, 27.4 us)
Async XLA Ops:
  7.2 13.2 %copy-start = (bf16[768,1536]{1,0:T(8,128)(2,1)S(1)}, bf16[768,1536]{1,0:T(8,128)(2,1)}, u32[]{:S(2)}) copy-start(bf16[768,1536]{1,0:T(8,128)(2,1)} %param.23) | copy-start | bytes 7077892
  7.2 7.3 copy-start.14
  7.2 7.3 copy-start.49
  7.2 67.1 %all-gather.5.cloned.1.call-start = ((), (), s32[]{:S(2)}) async-start(), calls=%async_computation.4 | async-start | bytes 3538944 | tf_op jit(solution)/shard_map/all_gather | solution.py:80
  7.3 4.0 collective-permute-start
  8.0 128.2 %all-gather.3.cloned.1.call-start = ((), (), s32[]{:S(2)}) async-start(), calls=%async_computation.2 | async-start | bytes 3538944 | tf_op jit(solution)/shard_map/all_gather | solution.py:103
  8.7 5.8 copy-start.11
  10.4 9.2 %copy-start.44 = (pred[256,256]{0,1:T(8,128)(4,1)}, pred[256,256]{0,1:T(8,128)(4,1)S(1)}, u32[]{:S(2)}) copy-start(pred[256,256]{0,1:T(8,128)(4,1)S(1)} %compare_and_fusion) | copy-start | bytes 196612
  11.2 4.5 copy-start.25
  11.2 10.2 %copy-start.16 = (bf16[128,1536]{1,0:T(8,128)(2,1)}, bf16[128,1536]{1,0:T(8,128)(2,1)S(1)}, u32[]{:S(2)}) copy-start(bf16[128,1536]{1,0:T(8,128)(2,1)S(1)} %collective-permute-done) | copy-start | bytes 1179652
  12.6 5.3 copy-start.62
  21.3 3.7 copy-start.46
  21.3 2.4 collective-permute-start.1
  25.9 227.9 %reduce-scatter.5.cloned.1.call-start = ((), (), s32[]{:S(2)}) async-start(), calls=%async_computation.5 | async-start | bytes 3538944 | tf_op jit(solution)/shard_map/reduce_scatter | solution.py:118
  26.0 41.3 %collective-permute-start.4 = (bf16[2,256,1536]{2,1,0:T(8,128)(2,1)}, bf16[2,256,1536]{2,1,0:T(8,128)(2,1)}, u32[]{:S(2)}, u32[]{:S(2)}) collective-permute-start(bf16[2,256,1536]{2,1,0:T(8,128)(2,1)} %param.26), channel_id=1, source_target_pairs={{0,1},{1,0},{2,3},{3,2},{4,5},{5,4},{6,7},{7,6},{8,9},{9,8},{10,11... | collective-permute-start | bytes 4718600 | tf_op jit(solution)/shard_map/ppermute | solution.py:16
  28.7 3.1 copy-start.57
  28.7 3.1 copy-start.58
  28.7 51.0 %collective-permute-start.2 = (bf16[2,1536,256]{1,2,0:T(8,128)(2,1)}, bf16[2,1536,256]{1,2,0:T(8,128)(2,1)}, u32[]{:S(2)}, u32[]{:S(2)}) collective-permute-start(bf16[2,1536,256]{1,2,0:T(8,128)(2,1)} %copy.77), channel_id=1, source_target_pairs={{0,1},{1,0},{2,3},{3,2},{4,5},{5,4},{6,7},{7,6},{8,9},{9,8},{10,11... | collective-permute-start | bytes 4718600 | tf_op jit(solution)/shard_map/ppermute | solution.py:16
  31.7 111.3 %collective-permute-start.3 = (bf16[2,1536,256]{1,2,0:T(8,128)(2,1)}, bf16[2,1536,256]{1,2,0:T(8,128)(2,1)}, u32[]{:S(2)}, u32[]{:S(2)}) collective-permute-start(bf16[2,1536,256]{1,2,0:T(8,128)(2,1)} %copy.79), channel_id=1, source_target_pairs={{0,1},{1,0},{2,3},{3,2},{4,5},{5,4},{6,7},{7,6},{8,9},{9,8},{10,11... | collective-permute-start | bytes 4718600 | tf_op jit(solution)/shard_map/ppermute | solution.py:16
  136.2 6.9 copy-start.13
  136.2 6.9 copy-start.65
  136.2 13.4 %slice-start = ((s8[6291456]{0:T(1024)(128)(4,1)}), s8[4194304]{0:T(1024)(128)(4,1)S(1)}, s32[]{:S(2)}) async-start(s8[6291456]{0:T(1024)(128)(4,1)} %bitcast.159), calls=%async_computation.8 | async-start | bytes 8388608
  143.0 6.6 slice-start.1
  158.9 8.6 %copy-start.69 = (bf16[2,1024,512]{1,2,0:T(8,128)(2,1)}, bf16[2,1024,512]{1,2,0:T(8,128)(2,1)S(1)}, u32[]{:S(2)}) copy-start(bf16[2,1024,512]{1,2,0:T(8,128)(2,1)S(1)} %get-tuple-element.65) | copy-start | bytes 6291460
  180.6 308.9 %all-reduce.5.cloned.1.call-start = ((), (), s32[]{:S(2)}) async-start(), calls=%async_computation.6 | async-start | bytes 12582912 | tf_op jit(solution)/shard_map/psum | solution.py:165
  257.1 1.8 collective-permute-start.5
  262.4 3.1 copy-start.8
  262.4 3.1 copy-start.45
  262.4 3.1 copy-start.54
  262.4 3.1 copy-start.68
  265.3 5.3 copy-start.47
  268.0 4.1 copy-start.35
  268.4 5.0 copy-start.18
  275.8 292.4 %reduce-scatter.3.cloned.1.call-start = ((), (), s32[]{:S(2)}) async-start(), calls=%async_computation.3 | async-start | bytes 3538944 | tf_op jit(solution)/shard_map/reduce_scatter | solution.py:119
  285.7 543.7 %all-reduce.7.cloned.1.call-start = ((), (), s32[]{:S(2)}) async-start(), calls=%async_computation.7 | async-start | bytes 22020096 | tf_op jit(solution)/shard_map/psum | solution.py:125
  286.0 6.9 copy-start.70
  292.7 10.6 %collective-permute-start.9 = (bf16[2,256,1536]{2,1,0:T(8,128)(2,1)S(1)}, bf16[2,256,1536]{2,1,0:T(8,128)(2,1)S(1)}, u32[]{:S(2)}, u32[]{:S(2)}) collective-permute-start(bf16[2,256,1536]{2,1,0:T(8,128)(2,1)S(1)} %split.101), channel_id=1, source_target_pairs={{0,1},{1,0},{2,3},{3,2},{4,5},{5,4},{6,7},{7,6},{8,9},{9,8},{10,11... | collective-permute-start | bytes 4718600 | tf_op jit(solution)/shard_map/ppermute | solution.py:16
  298.0 7.0 collective-permute-start.8
  303.0 3.8 collective-permute-start.7
  494.3 2.9 copy-start.51
  494.7 73.5 %copy-start.5 = (bf16[128,1536]{1,0:T(8,128)(2,1)S(1)}, bf16[128,1536]{1,0:T(8,128)(2,1)}, u32[]{:S(2)}) copy-start(bf16[128,1536]{1,0:T(8,128)(2,1)} %param.27) | copy-start | bytes 1179652
  494.7 73.5 %copy-start.6 = (bf16[128,1536]{1,0:T(8,128)(2,1)S(1)}, bf16[128,1536]{1,0:T(8,128)(2,1)}, u32[]{:S(2)}) copy-start(bf16[128,1536]{1,0:T(8,128)(2,1)} %reduce-scatter.5.cloned.1.call-done) | copy-start | bytes 1179652
  494.7 73.5 %copy-start.56 = (f32[128]{0:T(128)S(1)}, f32[128]{0:T(128)}, u32[]{:S(2)}) copy-start(f32[128]{0:T(128)} %copy-done.55) | copy-start | bytes 1540
  494.7 73.5 %copy-start.59 = (f32[128]{0:T(128)S(1)}, f32[128]{0:T(128)}, u32[]{:S(2)}) copy-start(f32[128]{0:T(128)} %get-tuple-element.83) | copy-start | bytes 1540
  494.8 73.5 %copy-start.61 = (f32[128]{0:T(128)S(1)}, f32[128]{0:T(128)}, u32[]{:S(2)}) copy-start(f32[128]{0:T(128)} %copy-done.60) | copy-start | bytes 1540
  494.8 2.4 collective-permute-start.6
  829.4 4.4 copy-start.10
  842.8 3.8 copy-start.1
  (42 other events, 69.4 us)
Sparse Core Ops, SparseCore 0:
  10.2 64.0 all-gather.4
  77.1 59.0 all-gather.2
  180.7 73.0 reduce-scatter.4
  275.9 213.5 all-reduce.4
  493.9 74.2 reduce-scatter.2
  572.6 256.7 all-reduce.6
